TPU v7x, 32 devices: a whole 2x2x4 slice. The times are simulated.
32 devices in a mesh: row: 4 (over x, core), col: 8 (over z, y).
Axes of the slice: x: 2, y: 2, z: 4, core: 2. Of those that a mesh axis runs over, the one named last changes fastest.
Arguments:
- coords: float32 [4, 4096], P(None, ('row', 'col')), may hold values from 0 to 1, as said below
- values: float32 [512, 4096], P(None, ('row', 'col')), may hold values from -6 to 6
- coarse_coords: float32 [4, 512], P(None, ('row', 'col')), may hold values from 0 to 1, as said below
- coarse_values: float32 [512, 512], P(None, ('row', 'col')), may hold values from -6 to 6
- fine_index: int32 [32, 128], P(('row', 'col')), may hold values from 0 to 127, as said below
- coarse_index: int32 [32, 384], P(('row', 'col')), may hold values from 0 to 511, as said below
- log_params: float32 [6], replicated, may hold values from -0.5 to 0.5
Outputs:
- step: float32 [6], replicated
- whitened: float32 [512, 4096], P(None, ('row', 'col'))
Inputs may be any that keep to these rules, and one draw needn't show every extreme that they name: `fine_index`: in each row the first 64 entries are distinct, and so are the last 64. `coarse_index`: the entries of each row are distinct; in each row at most 16 entries lie in one tile (j // 16), and some tile holds exactly 16 of them. `coarse_coords`: coarse point j lies in tile j // 16; for tile (r, c) its longitude lies in [c / 8, (c + 1) / 8) and its latitude in [r / 4, (r + 1) / 4), elevation and time in [0, 1). `coords`: fine point p lies in tile p // 128, placed as for the coarse points.
All inputs are finite; a program needn't handle non-finite values.
Results may differ from a plain program's by a relative error of at most 0.0003.
Values sent between devices are 32-bit elements; how exact they have to be, the bound alone decides.
A program may use at most 192 MiB of HBM per device.

v0:
```python
import math
import jax
import jax.numpy as jnp
from jax import lax
from jax.sharding import PartitionSpec as P

HIGH = lax.Precision.HIGHEST
ROOT_FIVE = math.sqrt(5.0)
NUGGET = 0.2
RANGE_BASE = (0.5, 0.5, 0.5, 0.5)


def shifted(value, axis, steps):
    count = lax.axis_size(axis)
    first, last = (max(0, -steps), min(count, count - steps))
    return lax.ppermute(value, axis, [(source, source + steps) for source in range(first, last)])


def passed_along(block, axis, distance):
    devices = range(lax.axis_size(axis))
    route = [((i - distance) % len(devices), i) for i in devices]
    return lax.ppermute(block, axis, route)


def local_covariance(joint_coords, live, theta):
    count = joint_coords.shape[1]
    scale = jnp.exp(theta[1:5]) * jnp.array(RANGE_BASE)
    scaled = joint_coords / scale[:, None]
    diff = scaled[:, :, None] - scaled[:, None, :]
    squares = diff * diff
    dist = jnp.sqrt(jnp.sum(squares, axis=0))
    root = ROOT_FIVE * dist
    decay = jnp.exp(-root)
    variance = jnp.exp(theta[0])
    kernel = variance * (1.0 + root + root * root / 3.0) * decay
    common = variance * (5.0 / 3.0) * (1.0 + root) * decay
    paired = live[:, None] * live[None, :]
    ident = jnp.eye(count, dtype=jnp.float32)
    nugget = NUGGET * jnp.exp(theta[5])
    cov = paired * kernel + (live * nugget + 1.0 - live)[:, None] * ident
    derivs = jnp.concatenate(
        [
            (paired * kernel)[None],
            (paired * common)[None] * squares,
            ((live * nugget)[:, None] * ident)[None],
        ],
        axis=0,
    )
    return (cov, derivs)


def fisher_terms(cov, derivs, lead, reps):
    count = cov.shape[0]
    ident = jnp.eye(count, dtype=jnp.float32)
    factor = jnp.linalg.cholesky(cov)
    inverse = jax.scipy.linalg.solve_triangular(factor, ident, lower=True)
    joint_prec = jnp.dot(inverse.T, inverse, precision=HIGH)
    lead_inv = inverse[:lead, :lead]
    lead_prec = jnp.dot(lead_inv.T, lead_inv, precision=HIGH)
    joint_prod = jnp.einsum("ab,ibc->iac", joint_prec, derivs, precision=HIGH)
    lead_prod = jnp.einsum("ab,ibc->iac", lead_prec, derivs[:, :lead, :lead], precision=HIGH)
    joint_fish = jnp.einsum("iab,jba->ij", joint_prod, joint_prod, precision=HIGH)
    lead_fish = jnp.einsum("iab,jba->ij", lead_prod, lead_prod, precision=HIGH)
    fisher = reps * 0.5 * (joint_fish - lead_fish)
    traces = jnp.trace(joint_prod, axis1=1, axis2=2) - jnp.trace(lead_prod, axis1=1, axis2=2)
    return (inverse, fisher, traces)


def score_terms(inverse, derivs, joint_values, traces, lead, reps):
    white = jnp.dot(joint_values, inverse.T, precision=HIGH)
    alpha = jnp.dot(white, inverse, precision=HIGH)
    lead_alpha = jnp.dot(white[:, :lead], inverse[:lead, :lead], precision=HIGH)
    joint_quad = jnp.sum(
        jnp.einsum("rn,inm->irm", alpha, derivs, precision=HIGH) * alpha[None], axis=(1, 2)
    )
    lead_quad = jnp.sum(
        jnp.einsum("rn,inm->irm", lead_alpha, derivs[:, :lead, :lead], precision=HIGH)
        * lead_alpha[None],
        axis=(1, 2),
    )
    grad = 0.5 * (joint_quad - lead_quad) - 0.5 * reps * traces
    return (grad, white[:, lead:])


def body(coords, values, coarse_coords, coarse_values, fine_index, coarse_index, log_params):
    half = fine_index.shape[1] // 2
    reps = values.shape[0]
    block_size = coords.shape[1]
    pick_upper = fine_index[0, :half]
    pick_left = fine_index[0, half:]
    wanted = coarse_index[0]
    num_coarse = wanted.shape[0]
    lead = num_coarse + 2 * half
    upper_coords, upper_values = shifted((coords, values), "row", 1)
    left_coords, left_values = passed_along((coords, values), "col", 1)
    upper_coords = jnp.take(upper_coords, pick_upper, axis=1)
    upper_values = jnp.take(upper_values, pick_upper, axis=1)
    left_coords = jnp.take(left_coords, pick_left, axis=1)
    left_values = jnp.take(left_values, pick_left, axis=1)
    piece_coords = lax.all_gather(coarse_coords, ("row", "col"), axis=1, tiled=True)
    piece_values = lax.all_gather(coarse_values, ("row", "col"), axis=1, tiled=True)
    width = piece_coords.shape[1]
    onehot = (wanted[None, :] == jnp.arange(width, dtype=jnp.int32)[:, None]).astype(jnp.float32)
    picked_coords = jnp.dot(piece_coords, onehot, precision=HIGH)
    picked_values = jnp.dot(piece_values, onehot, precision=HIGH)
    upper_live = (lax.axis_index("row") > 0).astype(jnp.float32)
    joint_coords = jnp.concatenate([picked_coords, upper_coords, left_coords, coords], axis=1)
    joint_values = jnp.concatenate([picked_values, upper_values, left_values, values], axis=1)
    live = jnp.concatenate(
        [
            jnp.ones((num_coarse,), jnp.float32),
            upper_live * jnp.ones((half,), jnp.float32),
            jnp.ones((half + block_size,), jnp.float32),
        ]
    )
    cov, derivs = local_covariance(joint_coords, live, log_params)
    inverse, fisher, traces = fisher_terms(cov, derivs, lead, reps)
    grad, white = score_terms(inverse, derivs, joint_values, traces, lead, reps)
    grad, fisher = lax.psum((grad, fisher), ("row", "col"))
    step = jax.scipy.linalg.cho_solve((jnp.linalg.cholesky(fisher), True), grad)
    return (step, white)


def solution(mesh):
    in_specs = (
        P(None, ("row", "col")),
        P(None, ("row", "col")),
        P(None, ("row", "col")),
        P(None, ("row", "col")),
        P(("row", "col"), None),
        P(("row", "col"), None),
        P(),
    )
    out_specs = (P(), P(None, ("row", "col")))
    return jax.shard_map(body, mesh=mesh, in_specs=in_specs, out_specs=out_specs, check_vma=False)
```

profile of v0, /device:TPU:14, one launch (start us, length us, event | category | flops | bytes accessed | tf_op | source)
XLA Modules:
  0.0 582.0 jit_solution(4296260236476704063)
XLA Ops:
  9.6 1.9 collective-permute-start
  14.8 1.9 collective-permute-start.2
  21.9 61.8 %all-gather = f32[32,16,4]{1,2,0:T(4,128)S(1)} all-gather(f32[1,16,4]{1,2,0:T(4,128)S(1)} %bitcast.157), channel_id=1, replica_groups=mesh['row'=4,'col'=8] {'row','col'}, dimensions={0}, use_global_device_ids=true | all-gather | bytes 8448 | tf_op jit(solution)/shard_map/all_gather | solution.py:100
  90.9 3.2 negate_exponential_fusion
  95.2 2.1 copy.63
  100.1 2.7 copy.66
  102.8 3.2 copy.65
  106.0 2.3 add_multiply_fusion.1
  109.5 11.7 %cholesky.146 = f32[128,128]{1,0:T(8,128)S(1)} custom-call(f32[128,128]{1,0:T(8,128)S(1)} %cholesky.372), custom_call_target="Cholesky" | custom-call | tf_op jit(solution)/shard_map/jit(cholesky)/cholesky | solution.py:55
  123.4 11.3 %custom-call.49 = f32[1,128,128]{1,2,0:T(8,128)} custom-call(f32[1,128,128]{2,1,0:T(8,128)} %get-tuple-element.43), custom_call_target="InvertDiagBlocksLowerTriangular" | custom-call | tf_op jit(solution)/shard_map/jit(cholesky)/cholesky | solution.py:55
  137.7 13.2 %cholesky.171 = f32[128,128]{1,0:T(8,128)} custom-call(f32[128,128]{1,0:T(8,128)} %cholesky.376), custom_call_target="Cholesky" | custom-call | tf_op jit(solution)/shard_map/jit(cholesky)/cholesky | solution.py:55
  150.8 2.0 select_reduce_fusion.5
  152.9 11.4 %custom-call.50 = f32[1,128,128]{1,2,0:T(8,128)} custom-call(f32[1,128,128]{2,1,0:T(8,128)} %get-tuple-element.40), custom_call_target="InvertDiagBlocksLowerTriangular" | custom-call | tf_op jit(solution)/shard_map/jit(cholesky)/cholesky | solution.py:55
  167.3 13.2 %cholesky.317 = f32[128,128]{1,0:T(8,128)} custom-call(f32[128,128]{1,0:T(8,128)} %cholesky.381), custom_call_target="Cholesky" | custom-call | tf_op jit(solution)/shard_map/jit(cholesky)/cholesky | solution.py:55
  180.5 2.0 select_reduce_fusion.4
  182.5 11.3 %custom-call.51 = f32[1,128,128]{1,2,0:T(8,128)} custom-call(f32[1,128,128]{2,1,0:T(8,128)} %get-tuple-element.37), custom_call_target="InvertDiagBlocksLowerTriangular" | custom-call | tf_op jit(solution)/shard_map/jit(cholesky)/cholesky | solution.py:55
  196.7 13.4 %cholesky.336 = f32[128,128]{1,0:T(8,128)} custom-call(f32[128,128]{1,0:T(8,128)} %cholesky.386), custom_call_target="Cholesky" | custom-call | tf_op jit(solution)/shard_map/jit(cholesky)/cholesky | solution.py:55
  210.0 2.1 select_reduce_fusion.3
  212.1 11.3 %custom-call.52 = f32[1,128,128]{1,2,0:T(8,128)} custom-call(f32[1,128,128]{2,1,0:T(8,128)} %get-tuple-element.34), custom_call_target="InvertDiagBlocksLowerTriangular" | custom-call | tf_op jit(solution)/shard_map/jit(cholesky)/cholesky | solution.py:55
  225.4 12.5 %cholesky.353 = f32[128,128]{1,0:T(8,128)S(1)} custom-call(f32[128,128]{1,0:T(8,128)} %convolution_subtract_fusion.6), custom_call_target="Cholesky" | custom-call | tf_op jit(solution)/shard_map/jit(cholesky)/cholesky | solution.py:55
  247.0 13.1 %while.1 = (s32[]{:T(128)}, f32[640,640]{1,0:T(8,128)S(1)}, s32[5,2]{0,1:T(2,128)S(1)}, f32[5,128,128]{2,1,0:T(8,128)}, s32[]{:T(128)}) while((s32[]{:T(128)}, f32[640,640]{1,0:T(8,128)S(1)}, s32[5,2]{0,1:T(2,128)S(1)}, f32[5,128,128]{2,1,0:T(8,128)}, s32[]{:T(128)}) %tuple.51), condition=%wide.while_cond, body=%wide.while_body.sunk | while | flops 2 | bytes 132205 | solution.py:56
  247.6 2.0 bitcast_dynamic-update-slice_fusion.2
  250.3 2.0 bitcast_dynamic-update-slice_fusion.2
  252.9 2.0 bitcast_dynamic-update-slice_fusion.2
  255.5 2.0 bitcast_dynamic-update-slice_fusion.2
  258.1 2.0 bitcast_dynamic-update-slice_fusion.2
  261.3 50.9 %custom-call.53 = f32[5,128,128]{1,2,0:T(8,128)} custom-call(f32[5,128,128]{2,1,0:T(8,128)} %get-tuple-element.11), custom_call_target="InvertDiagBlocksLowerTriangular" | custom-call | tf_op jit(solution)/shard_map/jit(_solve_triangular)/triangular_solve | solution.py:56
  318.3 1.9 convolution_subtract_fusion.2
  320.7 2.0 fusion.30
  322.7 2.9 convolution_bitcast_fusion.1
  326.1 6.2 %fusion.100 = f32[640,640]{1,0:T(8,128)} fusion(f32[640,640]{1,0:T(8,128)S(1)} %convolution_dynamic-update-slice_fusion), kind=kOutput, calls=%fused_computation.189 | convolution fusion | flops 3145728000 | bytes 3276800 | tf_op jit(solution)/shard_map/dot_general | solution.py:57
  332.4 3.8 fusion.7
  336.2 2.9 copy.64
  339.0 30.9 %select_reduce_fusion = (f32[6]{0:T(128)S(1)}, f32[6,640,640]{1,2,0:T(8,128)}) fusion(pred[640,640]{0,1:T(8,128)(4,1)S(1)} %copy-done.22, f32[640,640]{1,0:T(8,128)} %fusion.100, f32[1,640,640]{1,2,0:T(8,128)S(1)} %copy-done.4, f32[4,640,640]{1,2,0:T(8,128)} %fusion.7, f32[1,640,640]{1,2,0:T(8,128)} %copy.64), kind=kOutput, calls=%fused_computation.9 | convolution fusion | flops 18884198400 | bytes 21708824 | tf_op jit(solution)/shard_map/ab,ibc->iac/dot_general | solution.py:60
  369.9 14.5 %copy.67 = f32[6,640,640]{2,0,1:T(8,128)} copy(f32[6,640,640]{1,2,0:T(8,128)} %get-tuple-element.63) | data formatting | bytes 19660800 | tf_op jit(solution)/shard_map/ab,ibc->iac/transpose | solution.py:60
  384.4 16.0 %select_reduce_fusion.1 = (f32[6]{0:T(128)S(1)}, f32[6,512,512]{1,2,0:T(8,128)}) fusion(pred[512,512]{0,1:T(8,128)(4,1)S(1)} %copy-done.17, f32[512,512,1]{1,0,2:T(8,128)S(1)} %copy-done.18, f32[1,640,640]{1,2,0:T(8,128)S(1)} %copy-done.4, f32[4,640,640]{1,2,0:T(8,128)} %fusion.7, f32[1,640,640]{1,2,0:T(8,128)} %copy.64), kind=kOutput, calls=%fused_computation.22 | convolution fusion | flops 9669967872 | bytes 17432600 | tf_op jit(solution)/shard_map/ab,ibc->iac/dot_general | solution.py:61
  400.4 9.8 %copy.69 = f32[6,512,512]{2,0,1:T(8,128)} copy(f32[6,512,512]{1,2,0:T(8,128)} %get-tuple-element.65) | data formatting | bytes 12582912 | tf_op jit(solution)/shard_map/ab,ibc->iac/transpose | solution.py:61
  410.2 34.7 %fusion.36 = f32[6,6]{0,1:T(8,128)S(1)} fusion(f32[6,640,640]{2,0,1:T(8,128)} %copy.67, f32[6,640,640]{1,2,0:T(8,128)} %get-tuple-element.63), kind=kOutput, calls=%fused_computation.72 | convolution fusion | flops 176947200 | bytes 19660944 | tf_op jit(solution)/shard_map/iab,jba->ij/dot_general | solution.py:62
  445.0 18.9 %fusion.42 = f32[6,6]{0,1:T(8,128)S(1)} fusion(f32[6,6]{0,1:T(8,128)S(1)} %fusion.36, f32[6,512,512]{2,0,1:T(8,128)S(1)} %copy-done, f32[6,512,512]{1,2,0:T(8,128)S(1)} %bitcast.156), kind=kOutput, calls=%fused_computation.74 | convolution fusion | flops 113246280 | bytes 12583200 | tf_op jit(solution)/shard_map/iab,jba->ij/dot_general | solution.py:63
  466.8 2.3 convolution_bitcast_fusion.2
  469.0 7.4 %fusion.21 = f32[512,640]{1,0:T(8,128)S(1)} fusion(f32[640,640]{1,0:T(8,128)S(1)} %copy-done.2, f32[512,128]{0,1:T(8,128)} %copy.75, f32[512,64]{0,1:T(8,128)S(1)} %select_bitcast_fusion, f32[512,64]{0,1:T(8,128)S(1)} %select_bitcast_fusion.1, f32[512,384]{0,1:T(8,128)S(1)} %convolution_bitcast_fusion.2), kind=kOutput, calls=%fused_computation.48 | convolution fusion | flops 2517565440 | bytes 4259840 | tf_op jit(solution)/shard_map/dot_general | solution.py:70
  476.5 4.8 fusion.101
  481.3 3.0 fusion.45
  484.3 2.9 copy.78
  487.2 21.7 %fusion.4 = f32[6]{0:T(128)S(1)} fusion(f32[512,640]{0,1:T(8,128)} %copy.78, f32[1,640,640]{1,2,0:T(8,128)S(1)} %copy-done.5, f32[4,640,640]{1,2,0:T(8,128)} %fusion.7, f32[1,640,640]{1,2,0:T(8,128)} %copy.64, f32[512,640]{1,0:T(8,128)} %fusion.101), kind=kOutput, calls=%fused_computation.13 | convolution fusion | flops 15108341760 | bytes 12451864 | tf_op jit(solution)/shard_map/rn,inm->irm/dot_general | solution.py:74
  508.9 2.6 copy.79
  511.5 14.1 %fusion.9 = f32[6]{0:T(128)S(1)} fusion(f32[512,512]{0,1:T(8,128)} %copy.79, f32[1,640,640]{1,2,0:T(8,128)S(1)} %copy-done.5, f32[4,640,640]{1,2,0:T(8,128)} %fusion.7, f32[1,640,640]{1,2,0:T(8,128)} %copy.64, f32[512,512]{1,0:T(8,128)} %fusion.45), kind=kOutput, calls=%fused_computation.21 | convolution fusion | flops 9669967872 | bytes 11927576 | tf_op jit(solution)/shard_map/rn,inm->irm/dot_general | solution.py:77
  526.3 45.2 %all-reduce.1 = (f32[6,6]{0,1:T(8,128)S(1)}, f32[6]{0:T(128)S(1)}) all-reduce(f32[6,6]{0,1:T(8,128)S(1)} %fusion.42, f32[6]{0:T(128)S(1)} %multiply_subtract_fusion), channel_id=1, replica_groups=mesh['row'=4,'col'=8] {'row','col'}, use_global_device_ids=true, to_apply=%region_11.13 | all-reduce | flops 42 | bytes 336 | tf_op jit(solution)/shard_map/psum | solution.py:119
  (178 shorter events, 58.6 us)
Async XLA Ops:
  7.2 14.6 %copy-start.36 = (s32[1,128]{1,0:T(1,128)S(1)}, s32[1,128]{1,0:T(1,128)}, u32[]{:S(2)}) copy-start(s32[1,128]{1,0:T(1,128)} %param.16) | copy-start | bytes 1540
  7.2 14.7 %copy-start.35 = (f32[4,16]{1,0:T(4,128)S(1)}, f32[4,16]{1,0:T(4,128)}, u32[]{:S(2)}) copy-start(f32[4,16]{1,0:T(4,128)} %param.14) | copy-start | bytes 772
  7.2 76.6 %copy-start.37 = (s32[1,384]{1,0:T(1,128)S(1)}, s32[1,384]{1,0:T(1,128)}, u32[]{:S(2)}) copy-start(s32[1,384]{1,0:T(1,128)} %param.17) | copy-start | bytes 4612
  7.2 459.5 %all-gather.3.cloned.1.call-start = ((), (), s32[]{:S(2)}) async-start(), calls=%async_computation | async-start | bytes 1081344 | tf_op jit(solution)/shard_map/all_gather | solution.py:101
  8.0 80.7 %collective-permute-start.1 = (f32[4,128]{0,1:T(8,128)S(1)}, f32[4,128]{0,1:T(8,128)S(1)}, u32[]{:S(2)}, u32[]{:S(2)}) collective-permute-start(f32[4,128]{0,1:T(8,128)S(1)} %copy.58), channel_id=1, source_target_pairs={{7,0},{0,1},{1,2},{2,3},{3,4},{4,5},{5,6},{6,7},{15,8},{8,9},{9,10... | collective-permute-start | bytes 6152 | tf_op jit(solution)/shard_map/ppermute | solution.py:22
  9.6 79.8 %collective-permute-start = (f32[4,128]{0,1:T(8,128)S(1)}, f32[4,128]{0,1:T(8,128)S(1)}, u32[]{:S(2)}, u32[]{:S(2)}) collective-permute-start(f32[4,128]{0,1:T(8,128)S(1)} %copy.58), channel_id=1, source_target_pairs={{0,8},{8,16},{16,24},{1,9},{9,17},{17,25},{2,10},{10,18},{18,26},{... | collective-permute-start | bytes 6152 | tf_op jit(solution)/shard_map/ppermute | solution.py:16
  13.3 450.6 %collective-permute-start.3 = (f32[512,128]{0,1:T(8,128)}, f32[512,128]{0,1:T(8,128)}, u32[]{:S(2)}, u32[]{:S(2)}) collective-permute-start(f32[512,128]{0,1:T(8,128)} %copy.75), channel_id=1, source_target_pairs={{7,0},{0,1},{1,2},{2,3},{3,4},{4,5},{5,6},{6,7},{15,8},{8,9},{9,10... | collective-permute-start | bytes 786440 | tf_op jit(solution)/shard_map/ppermute | solution.py:22
  14.8 450.9 %collective-permute-start.2 = (f32[512,128]{0,1:T(8,128)}, f32[512,128]{0,1:T(8,128)S(1)}, u32[]{:S(2)}, u32[]{:S(2)}) collective-permute-start(f32[512,128]{0,1:T(8,128)} %copy.75), channel_id=1, source_target_pairs={{0,8},{8,16},{16,24},{1,9},{9,17},{17,25},{2,10},{10,18},{18,26},{... | collective-permute-start | bytes 786440 | tf_op jit(solution)/shard_map/ppermute | solution.py:16
  16.9 69.8 %copy-start.14 = (pred[640,640]{1,0:T(32,128)(4,1)}, pred[640,640]{1,0:T(32,128)(4,1)S(1)}, u32[]{:S(2)}) copy-start(pred[640,640]{1,0:T(32,128)(4,1)S(1)} %iota_compare_fusion.1) | copy-start | bytes 1228804
  20.3 69.8 %copy-start.26 = (f32[4,128]{1,0:T(4,128)S(1)}, f32[4,128]{1,0:T(4,128)}, u32[]{:S(2)}) copy-start(f32[4,128]{1,0:T(4,128)} %param.12) | copy-start | bytes 6148
  21.8 69.0 %copy-start.31 = (pred[64]{0:T(512)(128)(4,1)}, pred[64]{0:T(512)(128)(4,1)S(1)}, u32[]{:S(2)}) copy-start(pred[64]{0:T(512)(128)(4,1)S(1)} %get-tuple-element.22) | copy-start | bytes 196
  21.8 69.0 %copy-start.33 = (pred[64]{0:T(512)(128)(4,1)}, pred[64]{0:T(512)(128)(4,1)S(1)}, u32[]{:S(2)}) copy-start(pred[64]{0:T(512)(128)(4,1)S(1)} %get-tuple-element.50) | copy-start | bytes 196
  21.8 68.2 %copy-start.30 = (s32[1024]{0:T(1024)}, s32[1024]{0:T(1024)S(1)}, u32[]{:S(2)}) copy-start(s32[1024]{0:T(1024)S(1)} %pad_clamp_fusion) | copy-start | bytes 12292
  21.9 68.2 %copy-start.29 = (s32[1024]{0:T(1024)}, s32[1024]{0:T(1024)S(1)}, u32[]{:S(2)}) copy-start(s32[1024]{0:T(1024)S(1)} %pad_clamp_fusion.1) | copy-start | bytes 12292
  83.8 7.1 %copy-start.27 = (s32[384]{0:T(512)}, s32[384]{0:T(512)S(1)}, u32[]{:S(2)}) copy-start(s32[384]{0:T(512)S(1)} %reduce.36) | copy-start | bytes 4612
  102.8 3.2 copy-start.25
  108.4 1.2 copy-start.9
  109.5 25.2 %copy-start.10 = (f32[640,640]{1,0:T(8,128)S(1)}, f32[640,640]{1,0:T(8,128)}, u32[]{:S(2)}) copy-start(f32[640,640]{1,0:T(8,128)} %copy-done.9) | copy-start | bytes 4915204
  121.2 0.6 copy-start.24
  136.3 0.7 copy-start.19
  166.0 0.7 copy-start.20
  195.4 0.7 copy-start.21
  246.3 0.7 copy-start.38
  260.1 1.2 copy-start.11
  260.1 56.1 %copy-start.8 = (f32[640,640]{1,0:T(8,128)S(1)}, f32[640,640]{1,0:T(8,128)}, u32[]{:S(2)}) copy-start(f32[640,640]{1,0:T(8,128)} %fusion.53) | copy-start | bytes 4915204
  313.4 4.4 copy-start.23
  316.2 6.5 %copy-start.6 = (f32[128,640]{1,0:T(8,128)}, f32[128,640]{1,0:T(8,128)S(1)}, u32[]{:S(2)}) copy-start(f32[128,640]{1,0:T(8,128)S(1)} %get-tuple-element.57) | copy-start | bytes 983044
  318.3 4.4 copy-start.12
  320.7 5.0 copy-start.15
  326.1 6.2 %copy-start.1 = (f32[640,640]{1,0:T(8,128)}, f32[640,640]{1,0:T(8,128)S(1)}, u32[]{:S(2)}) copy-start(f32[640,640]{1,0:T(8,128)S(1)} %convolution_dynamic-update-slice_fusion) | copy-start | bytes 4915204
  326.1 6.2 %copy-start.3 = (f32[640,640]{0,1:T(8,128)S(1)}, f32[640,640]{0,1:T(8,128)}, u32[]{:S(2)}) copy-start(f32[640,640]{0,1:T(8,128)} %get-tuple-element.30) | copy-start | bytes 4915204
  336.1 2.9 copy-start.4
  336.1 2.9 copy-start.22
  369.9 14.5 %copy-start.17 = (pred[512,512]{0,1:T(8,128)(4,1)S(1)}, pred[512,512]{0,1:T(8,128)(4,1)}, u32[]{:S(2)}) copy-start(pred[512,512]{0,1:T(8,128)(4,1)} %iota_compare_fusion.4) | copy-start | bytes 786436
  369.9 14.5 %copy-start.18 = (f32[512,512,1]{1,0,2:T(8,128)S(1)}, f32[512,512,1]{1,0,2:T(8,128)}, u32[]{:S(2)}) copy-start(f32[512,512,1]{1,0,2:T(8,128)} %convolution_bitcast_fusion.1) | copy-start | bytes 3145732
  400.4 44.5 %slice-start = ((s8[6291456]{0:T(1024)(128)(4,1)}), s8[2097152]{0:T(1024)(128)(4,1)S(1)}, s32[]{:S(2)}) async-start(s8[6291456]{0:T(1024)(128)(4,1)} %bitcast.155), calls=%async_computation.1 | async-start | bytes 4194304
  410.2 34.8 %slice-start.1 = ((s8[6291456]{0:T(1024)(128)(4,1)}), s8[4194304]{0:T(1024)(128)(4,1)S(1)}, s32[]{:S(2)}) async-start(s8[6291456]{0:T(1024)(128)(4,1)} %bitcast.155), calls=%async_computation.2 | async-start | bytes 8388608
  410.2 34.8 %copy-start = (f32[6,512,512]{2,0,1:T(8,128)S(1)}, f32[6,512,512]{2,0,1:T(8,128)}, u32[]{:S(2)}) copy-start(f32[6,512,512]{2,0,1:T(8,128)} %copy.69) | copy-start | bytes 18874372
  465.7 0.8 copy-start.34
  465.7 0.9 copy-start.32
  465.7 1.0 copy-start.28
  466.5 2.5 copy-start.2
  476.5 4.8 copy-start.7
  476.5 4.8 copy-start.13
  476.5 4.8 copy-start.16
  484.3 2.9 copy-start.5
Sparse Core Ops, SparseCore 0:
  16.9 53.3 all-gather.2
where the time goes:
time: 589 us; the launch traced here: 582 us
  other arithmetic  193 us (33%)
  matrix products  182 us (31%)
  blocking collectives  107 us (18%)
  local copies, waits for them, and re-layouts  73.2 us (12%)
  between operations  19.7 us (3%)
  starting transfers between devices  6.94 us (1%)
    another operation x19, other arithmetic, fisher_terms(): factor = jnp.linalg.cholesky(cov)  121 us
    all_gather x1, blocking collectives, body(): lax.all_gather(coarse_coords, ('row', 'col'), axis=1, tiled=True)  61.8 us
    another operation x3, other arithmetic, fisher_terms(): inverse = jax.scipy.linalg.solve_triangular(factor, ident, lower=True)  51.7 us
    psum x1, blocking collectives, body(): grad, fisher = lax.psum((grad, fisher), ('row', 'col'))  45.2 us
    dot_general x1, matrix products, fisher_terms(): jnp.einsum('iab,jba->ij', joint_prod, joint_prod, precision=HIGH)  34.7 us
    dot_general x1, matrix products, fisher_terms(): joint_prod = jnp.einsum('ab,ibc->iac', joint_prec, derivs, precision=HIGH)  30.9 us
    dot_general x1, matrix products, score_terms(): jnp.einsum('rn,inm->irm', alpha, derivs, precision=HIGH) * alpha[None]  21.7 us
    dot_general x1, matrix products, fisher_terms(): lead_fish = jnp.einsum('iab,jba->ij', lead_prod, lead_prod, precision=HIGH)  18.9 us
  transfers between devices with their start and end apart: 5, of which 0 were waited for; matrix products, arithmetic and copies ran while one was open for 65% of the time, Pallas kernels for 0%

commit v1 on v0

--- a/solution.py
+++ b/solution.py
@@ -97,8 +97,16 @@
     upper_values = jnp.take(upper_values, pick_upper, axis=1)
     left_coords = jnp.take(left_coords, pick_left, axis=1)
     left_values = jnp.take(left_values, pick_left, axis=1)
-    piece_coords = lax.all_gather(coarse_coords, ("row", "col"), axis=1, tiled=True)
-    piece_values = lax.all_gather(coarse_values, ("row", "col"), axis=1, tiled=True)
+    piece_coords, piece_values = jnp.split(
+        lax.all_gather(
+            jnp.concatenate([coarse_coords, coarse_values], axis=0),
+            ("row", "col"),
+            axis=1,
+            tiled=True,
+        ),
+        [coarse_coords.shape[0]],
+        axis=0,
+    )
     width = piece_coords.shape[1]
     onehot = (wanted[None, :] == jnp.arange(width, dtype=jnp.int32)[:, None]).astype(jnp.float32)
     picked_coords = jnp.dot(piece_coords, onehot, precision=HIGH)

time: 589 us -> 567 us (0.963)
  blocking collectives: 107 us -> 40 us
  waiting for transfers between devices: 0.05 us -> 40.5 us
    all_gather x1 -> x0, blocking collectives: 61.8 us -> none  [body(): lax.all_gather(coarse_coords, ('row', 'col'), axis=1, tiled=True)]
    all_gather x1, waiting for transfers between devices: 0.02 us -> 40.4 us  [body(): lax.all_gather(jnp.concatenate([coarse_coords, coarse_values], axis=0), (...]
  transfers between devices with their start and end apart: 5 -> 5, of which waited for: 0 -> 1; matrix products, arithmetic and copies ran while one was open for 65% -> 3% of each run, Pallas kernels for 0% -> 0%
where the time goes in v1:
time: 567 us; the launch traced here: 558 us
  other arithmetic  194 us (34%)
  matrix products  180 us (32%)
  local copies, waits for them, and re-layouts  76.6 us (14%)
  waiting for transfers between devices  40.5 us (7%)
  blocking collectives  40 us (7%)
  between operations  19.3 us (3%)
  starting transfers between devices  6.99 us (1%)
    another operation x19, other arithmetic, fisher_terms(): factor = jnp.linalg.cholesky(cov)  121 us
    another operation x3, other arithmetic, fisher_terms(): inverse = jax.scipy.linalg.solve_triangular(factor, ident, lower=True)  52.2 us
    all_gather x1, waiting for transfers between devices, body(): lax.all_gather(jnp.concatenate([coarse_coords, coarse_values], axis=0), (...  40.4 us
    psum x1, blocking collectives, body(): grad, fisher = lax.psum((grad, fisher), ('row', 'col'))  40 us
    dot_general x1, matrix products, fisher_terms(): jnp.einsum('iab,jba->ij', joint_prod, joint_prod, precision=HIGH)  35.2 us
    dot_general x1, matrix products, fisher_terms(): joint_prod = jnp.einsum('ab,ibc->iac', joint_prec, derivs, precision=HIGH)  31.4 us
    dot_general x1, matrix products, fisher_terms(): lead_fish = jnp.einsum('iab,jba->ij', lead_prod, lead_prod, precision=HIGH)  21.8 us
    dot_general x1, matrix products, score_terms(): jnp.einsum('rn,inm->irm', alpha, derivs, precision=HIGH) * alpha[None]  21.6 us
  transfers between devices with their start and end apart: 5, of which 1 were waited for; matrix products, arithmetic and copies ran while one was open for 3% of the time, Pallas kernels for 0%

profile of v1, /device:TPU:14, one launch (start us, length us, event | category | flops | bytes accessed | tf_op | source)
XLA Modules:
  0.0 557.9 jit_solution(3747743219382915508)
XLA Ops:
  9.6 1.9 collective-permute-start
  14.2 1.9 collective-permute-start.2
  32.0 40.4 %all-gather.2.cloned.1.call-done = f32[516,512]{0,1:T(8,128)} async-done(((f32[516,16]{0,1:T(8,128)}), f32[516,512]{0,1:T(8,128)}) %all-gather.2.cloned.1.call-update) | async-done | bytes 1056784 | tf_op jit(solution)/shard_map/all_gather | solution.py:101
  74.5 3.2 negate_exponential_fusion
  78.8 2.1 copy.41
  83.8 2.7 copy.44
  86.6 3.2 copy.43
  89.8 2.3 add_multiply_fusion.1
  93.4 11.7 %cholesky.146 = f32[128,128]{1,0:T(8,128)S(1)} custom-call(f32[128,128]{1,0:T(8,128)S(1)} %cholesky.372), custom_call_target="Cholesky" | custom-call | tf_op jit(solution)/shard_map/jit(cholesky)/cholesky | solution.py:55
  107.3 11.3 %custom-call.49 = f32[1,128,128]{1,2,0:T(8,128)} custom-call(f32[1,128,128]{2,1,0:T(8,128)} %get-tuple-element.43), custom_call_target="InvertDiagBlocksLowerTriangular" | custom-call | tf_op jit(solution)/shard_map/jit(cholesky)/cholesky | solution.py:55
  121.5 13.2 %cholesky.171 = f32[128,128]{1,0:T(8,128)} custom-call(f32[128,128]{1,0:T(8,128)} %cholesky.376), custom_call_target="Cholesky" | custom-call | tf_op jit(solution)/shard_map/jit(cholesky)/cholesky | solution.py:55
  134.7 2.0 select_reduce_fusion.5
  136.7 11.4 %custom-call.50 = f32[1,128,128]{1,2,0:T(8,128)} custom-call(f32[1,128,128]{2,1,0:T(8,128)} %get-tuple-element.40), custom_call_target="InvertDiagBlocksLowerTriangular" | custom-call | tf_op jit(solution)/shard_map/jit(cholesky)/cholesky | solution.py:55
  151.1 13.2 %cholesky.317 = f32[128,128]{1,0:T(8,128)} custom-call(f32[128,128]{1,0:T(8,128)} %cholesky.381), custom_call_target="Cholesky" | custom-call | tf_op jit(solution)/shard_map/jit(cholesky)/cholesky | solution.py:55
  164.3 2.0 select_reduce_fusion.4
  166.3 11.3 %custom-call.51 = f32[1,128,128]{1,2,0:T(8,128)} custom-call(f32[1,128,128]{2,1,0:T(8,128)} %get-tuple-element.37), custom_call_target="InvertDiagBlocksLowerTriangular" | custom-call | tf_op jit(solution)/shard_map/jit(cholesky)/cholesky | solution.py:55
  180.6 13.4 %cholesky.336 = f32[128,128]{1,0:T(8,128)} custom-call(f32[128,128]{1,0:T(8,128)} %cholesky.386), custom_call_target="Cholesky" | custom-call | tf_op jit(solution)/shard_map/jit(cholesky)/cholesky | solution.py:55
  193.9 2.0 select_reduce_fusion.3
  196.0 11.3 %custom-call.52 = f32[1,128,128]{1,2,0:T(8,128)} custom-call(f32[1,128,128]{2,1,0:T(8,128)} %get-tuple-element.34), custom_call_target="InvertDiagBlocksLowerTriangular" | custom-call | tf_op jit(solution)/shard_map/jit(cholesky)/cholesky | solution.py:55
  209.3 12.5 %cholesky.353 = f32[128,128]{1,0:T(8,128)S(1)} custom-call(f32[128,128]{1,0:T(8,128)} %convolution_subtract_fusion.6), custom_call_target="Cholesky" | custom-call | tf_op jit(solution)/shard_map/jit(cholesky)/cholesky | solution.py:55
  231.3 18.0 %while.1 = (s32[]{:T(128)}, f32[640,640]{1,0:T(8,128)}, s32[5,2]{0,1:T(2,128)S(1)}, f32[5,128,128]{2,1,0:T(8,128)}, s32[]{:T(128)}) while((s32[]{:T(128)}, f32[640,640]{1,0:T(8,128)}, s32[5,2]{0,1:T(2,128)S(1)}, f32[5,128,128]{2,1,0:T(8,128)}, s32[]{:T(128)}) %tuple.51), condition=%wide.while_cond, body=%wide.while_body.sunk | while | flops 2 | bytes 132205 | solution.py:56
  232.0 3.0 bitcast_dynamic-update-slice_fusion.2
  235.6 2.9 bitcast_dynamic-update-slice_fusion.2
  239.2 3.0 bitcast_dynamic-update-slice_fusion.2
  242.8 2.9 bitcast_dynamic-update-slice_fusion.2
  246.4 2.9 bitcast_dynamic-update-slice_fusion.2
  249.3 50.3 %custom-call.53 = f32[5,128,128]{1,2,0:T(8,128)S(1)} custom-call(f32[5,128,128]{2,1,0:T(8,128)} %get-tuple-element.11), custom_call_target="InvertDiagBlocksLowerTriangular" | custom-call | tf_op jit(solution)/shard_map/jit(_solve_triangular)/triangular_solve | solution.py:56
  304.5 1.8 convolution_subtract_fusion.2
  306.8 1.9 fusion.30
  308.7 2.9 convolution_bitcast_fusion.1
  312.1 6.2 %fusion.104 = f32[640,640]{1,0:T(8,128)} fusion(f32[640,640]{1,0:T(8,128)S(1)} %convolution_dynamic-update-slice_fusion), kind=kOutput, calls=%fused_computation.192 | convolution fusion | flops 3145728000 | bytes 3276800 | tf_op jit(solution)/shard_map/dot_general | solution.py:57
  320.0 3.8 fusion.21
  323.8 4.8 fusion.105
  328.6 2.8 fusion.45
  331.5 3.6 fusion.7
  335.0 2.2 copy.42
  337.3 31.4 %select_reduce_fusion = (f32[6]{0:T(128)S(1)}, f32[6,640,640]{1,2,0:T(8,128)}) fusion(pred[640,640]{0,1:T(8,128)(4,1)} %copy.59, f32[640,640]{1,0:T(8,128)} %fusion.104, f32[1,640,640]{1,2,0:T(8,128)S(1)} %copy-done.2, f32[4,640,640]{1,2,0:T(8,128)} %fusion.7, f32[1,640,640]{1,2,0:T(8,128)S(1)} %copy.42), kind=kOutput, calls=%fused_computation.9 | convolution fusion | flops 18884198400 | bytes 21708824 | tf_op jit(solution)/shard_map/ab,ibc->iac/dot_general | solution.py:60
  368.7 14.4 %copy.45 = f32[6,640,640]{2,0,1:T(8,128)} copy(f32[6,640,640]{1,2,0:T(8,128)} %get-tuple-element.63) | data formatting | bytes 19660800 | tf_op jit(solution)/shard_map/ab,ibc->iac/transpose | solution.py:60
  383.1 35.2 %fusion.36 = f32[6,6]{0,1:T(8,128)S(1)} fusion(f32[6,640,640]{2,0,1:T(8,128)} %copy.45, f32[6,640,640]{1,2,0:T(8,128)} %get-tuple-element.63), kind=kOutput, calls=%fused_computation.70 | convolution fusion | flops 176947200 | bytes 19660944 | tf_op jit(solution)/shard_map/iab,jba->ij/dot_general | solution.py:62
  418.4 16.0 %select_reduce_fusion.1 = (f32[6]{0:T(128)S(1)}, f32[6,512,512]{1,2,0:T(8,128)}) fusion(pred[512,512]{0,1:T(8,128)(4,1)S(1)} %iota_compare_fusion.4, f32[512,512,1]{1,0,2:T(8,128)S(1)} %copy-done.13, f32[1,640,640]{1,2,0:T(8,128)S(1)} %copy-done.3, f32[4,640,640]{1,2,0:T(8,128)S(1)} %bitcast.147, f32[1,640,640]{1,2,0:T(8,128)S(1)} %copy-done.6), kind=kOutput, calls=%fused_computation.22 | convolution fusion | flops 9669967872 | bytes 17432600 | tf_op jit(solution)/shard_map/ab,ibc->iac/dot_general | solution.py:61
  434.4 9.9 %copy.47 = f32[6,512,512]{2,0,1:T(8,128)} copy(f32[6,512,512]{1,2,0:T(8,128)} %get-tuple-element.65) | data formatting | bytes 12582912 | tf_op jit(solution)/shard_map/ab,ibc->iac/transpose | solution.py:61
  444.3 2.9 copy.57
  447.2 21.6 %fusion.4 = f32[6]{0:T(128)S(1)} fusion(f32[512,640]{0,1:T(8,128)} %copy.57, f32[1,640,640]{1,2,0:T(8,128)S(1)} %copy-done.4, f32[4,640,640]{1,2,0:T(8,128)} %fusion.7, f32[1,640,640]{1,2,0:T(8,128)S(1)} %copy-done.7, f32[512,640]{1,0:T(8,128)} %fusion.105), kind=kOutput, calls=%fused_computation.13 | convolution fusion | flops 15108341760 | bytes 12451864 | tf_op jit(solution)/shard_map/rn,inm->irm/dot_general | solution.py:74
  468.8 1.7 copy.58
  470.5 13.5 %fusion.9 = f32[6]{0:T(128)S(1)} fusion(f32[512,512]{0,1:T(8,128)S(1)} %copy.58, f32[1,640,640]{1,2,0:T(8,128)} %fusion.12, f32[4,640,640]{1,2,0:T(8,128)} %fusion.7, f32[1,640,640]{1,2,0:T(8,128)} %copy-done.5, f32[512,512]{1,0:T(8,128)} %fusion.45), kind=kOutput, calls=%fused_computation.21 | convolution fusion | flops 9669967872 | bytes 11927576 | tf_op jit(solution)/shard_map/rn,inm->irm/dot_general | solution.py:77
  484.1 21.8 %fusion.42 = f32[6,6]{0,1:T(8,128)S(1)} fusion(f32[6,6]{0,1:T(8,128)S(1)} %fusion.36, f32[6,512,512]{2,0,1:T(8,128)} %copy.47, f32[6,512,512]{1,2,0:T(8,128)S(1)} %bitcast.145), kind=kOutput, calls=%fused_computation.72 | convolution fusion | flops 113246280 | bytes 12583200 | tf_op jit(solution)/shard_map/iab,jba->ij/dot_general | solution.py:63
  505.9 1.7 slice.224
  507.6 40.0 %all-reduce.1 = (f32[6,6]{0,1:T(8,128)S(1)}, f32[6]{0:T(128)S(1)}) all-reduce(f32[6,6]{0,1:T(8,128)S(1)} %fusion.42, f32[6]{0:T(128)S(1)} %multiply_subtract_fusion), channel_id=1, replica_groups=mesh['row'=4,'col'=8] {'row','col'}, use_global_device_ids=true, to_apply=%region_11.13 | all-reduce | flops 42 | bytes 336 | tf_op jit(solution)/shard_map/psum | solution.py:127
  (162 shorter events, 60.3 us)
Async XLA Ops:
  7.2 16.4 %copy-start.25 = (f32[6]{0:T(128)S(1)}, f32[6]{0:T(128)}, u32[]{:S(2)}) copy-start(f32[6]{0:T(128)} %param.18) | copy-start | bytes 76
  7.2 65.3 %all-gather.2.cloned.1.call-start = ((), (), s32[]{:S(2)}) async-start(), calls=%async_computation | async-start | bytes 1351680 | tf_op jit(solution)/shard_map/all_gather | solution.py:101
  8.0 19.4 %collective-permute-start.1 = (f32[4,128]{0,1:T(8,128)S(1)}, f32[4,128]{0,1:T(8,128)S(1)}, u32[]{:S(2)}, u32[]{:S(2)}) collective-permute-start(f32[4,128]{0,1:T(8,128)S(1)} %copy.36), channel_id=1, source_target_pairs={{7,0},{0,1},{1,2},{2,3},{3,4},{4,5},{5,6},{6,7},{15,8},{8,9},{9,10... | collective-permute-start | bytes 6152 | tf_op jit(solution)/shard_map/ppermute | solution.py:22
  9.6 18.5 %collective-permute-start = (f32[4,128]{0,1:T(8,128)S(1)}, f32[4,128]{0,1:T(8,128)S(1)}, u32[]{:S(2)}, u32[]{:S(2)}) collective-permute-start(f32[4,128]{0,1:T(8,128)S(1)} %copy.36), channel_id=1, source_target_pairs={{0,8},{8,16},{16,24},{1,9},{9,17},{17,25},{2,10},{10,18},{18,26},{... | collective-permute-start | bytes 6152 | tf_op jit(solution)/shard_map/ppermute | solution.py:16
  12.6 16.2 %collective-permute-start.3 = (f32[512,128]{0,1:T(8,128)S(1)}, f32[512,128]{0,1:T(8,128)S(1)}, u32[]{:S(2)}, u32[]{:S(2)}) collective-permute-start(f32[512,128]{0,1:T(8,128)S(1)} %copy.53), channel_id=1, source_target_pairs={{7,0},{0,1},{1,2},{2,3},{3,4},{4,5},{5,6},{6,7},{15,8},{8,9},{9,10... | collective-permute-start | bytes 786440 | tf_op jit(solution)/shard_map/ppermute | solution.py:22
  14.2 16.3 %collective-permute-start.2 = (f32[512,128]{0,1:T(8,128)S(1)}, f32[512,128]{0,1:T(8,128)S(1)}, u32[]{:S(2)}, u32[]{:S(2)}) collective-permute-start(f32[512,128]{0,1:T(8,128)S(1)} %copy.53), channel_id=1, source_target_pairs={{0,8},{8,16},{16,24},{1,9},{9,17},{17,25},{2,10},{10,18},{18,26},{... | collective-permute-start | bytes 786440 | tf_op jit(solution)/shard_map/ppermute | solution.py:16
  22.2 3.3 copy-start.11
  23.5 3.2 copy-start.26
  26.8 45.7 %copy-start.22 = (s32[384]{0:T(512)}, s32[384]{0:T(512)S(1)}, u32[]{:S(2)}) copy-start(s32[384]{0:T(512)S(1)} %reduce.36) | copy-start | bytes 4612
  30.4 43.4 %copy-start.24 = (f32[4,128]{1,0:T(4,128)S(1)}, f32[4,128]{1,0:T(4,128)}, u32[]{:S(2)}) copy-start(f32[4,128]{1,0:T(4,128)} %param.12) | copy-start | bytes 6148
  86.6 3.3 copy-start.21
  92.1 1.2 copy-start.9
  93.4 25.2 %copy-start.10 = (f32[640,640]{1,0:T(8,128)S(1)}, f32[640,640]{1,0:T(8,128)}, u32[]{:S(2)}) copy-start(f32[640,640]{1,0:T(8,128)} %copy-done.9) | copy-start | bytes 4915204
  105.1 0.6 copy-start.20
  120.2 0.7 copy-start.17
  149.8 0.7 copy-start.18
  179.3 0.7 copy-start.19
  230.0 1.4 copy-start.27
  230.0 70.8 %copy-start.8 = (f32[640,640]{1,0:T(8,128)S(1)}, f32[640,640]{1,0:T(8,128)}, u32[]{:S(2)}) copy-start(f32[640,640]{1,0:T(8,128)} %fusion.55) | copy-start | bytes 4915204
  312.1 6.2 %copy-start.12 = (f32[516,512]{0,1:T(8,128)S(1)}, f32[516,512]{0,1:T(8,128)}, u32[]{:S(2)}) copy-start(f32[516,512]{0,1:T(8,128)} %all-gather.2.cloned.1.call-done) | copy-start | bytes 3170308
  312.1 6.2 %copy-start.23 = (s32[384]{0:T(512)S(1)}, s32[384]{0:T(512)}, u32[]{:S(2)}) copy-start(s32[384]{0:T(512)} %copy-done.22) | copy-start | bytes 4612
  318.3 1.7 copy-start.14
  318.3 1.7 copy-start.15
  318.3 1.7 copy-start.16
  323.8 4.8 copy-start
  328.6 2.8 copy-start.1
  335.0 2.2 copy-start.2
  337.2 31.4 %copy-start.5 = (f32[1,640,640]{1,2,0:T(8,128)}, f32[1,640,640]{1,2,0:T(8,128)S(1)}, u32[]{:S(2)}) copy-start(f32[1,640,640]{1,2,0:T(8,128)S(1)} %copy.42) | copy-start | bytes 4915204
  368.7 49.7 %slice-start.2 = ((s8[6553600]{0:T(1024)(128)(4,1)}), s8[2359296]{0:T(1024)(128)(4,1)S(1)}, s32[]{:S(2)}) async-start(s8[6553600]{0:T(1024)(128)(4,1)} %bitcast.146), calls=%async_computation.3 | async-start | bytes 4718592
  383.1 35.2 %slice-start.3 = ((s8[6553600]{0:T(1024)(128)(4,1)}), s8[4194304]{0:T(1024)(128)(4,1)S(1)}, s32[]{:S(2)}) async-start(s8[6553600]{0:T(1024)(128)(4,1)} %bitcast.146), calls=%async_computation.4 | async-start | bytes 8388608
  383.1 35.3 %copy-start.3 = (f32[1,640,640]{1,2,0:T(8,128)S(1)}, f32[1,640,640]{1,2,0:T(8,128)}, u32[]{:S(2)}) copy-start(f32[1,640,640]{1,2,0:T(8,128)} %fusion.12) | copy-start | bytes 4915204
  383.1 35.3 %copy-start.6 = (f32[1,640,640]{1,2,0:T(8,128)S(1)}, f32[1,640,640]{1,2,0:T(8,128)}, u32[]{:S(2)}) copy-start(f32[1,640,640]{1,2,0:T(8,128)} %copy-done.5) | copy-start | bytes 4915204
  383.1 35.3 %copy-start.13 = (f32[512,512,1]{1,0,2:T(8,128)S(1)}, f32[512,512,1]{1,0,2:T(8,128)}, u32[]{:S(2)}) copy-start(f32[512,512,1]{1,0,2:T(8,128)} %convolution_bitcast_fusion.1) | copy-start | bytes 3145732
  434.4 12.9 %copy-start.7 = (f32[1,640,640]{1,2,0:T(8,128)S(1)}, f32[1,640,640]{1,2,0:T(8,128)}, u32[]{:S(2)}) copy-start(f32[1,640,640]{1,2,0:T(8,128)} %copy-done.5) | copy-start | bytes 4915204
  444.3 2.9 copy-start.4
  468.8 15.3 %slice-start = ((s8[6291456]{0:T(1024)(128)(4,1)}), s8[2097152]{0:T(1024)(128)(4,1)S(1)}, s32[]{:S(2)}) async-start(s8[6291456]{0:T(1024)(128)(4,1)} %bitcast.144), calls=%async_computation.1 | async-start | bytes 4194304
  470.5 13.6 %slice-start.1 = ((s8[6291456]{0:T(1024)(128)(4,1)}), s8[4194304]{0:T(1024)(128)(4,1)S(1)}, s32[]{:S(2)}) async-start(s8[6291456]{0:T(1024)(128)(4,1)} %bitcast.144), calls=%async_computation.2 | async-start | bytes 8388608
Sparse Core Ops, SparseCore 0:
  18.4 53.9 all-gather.1
